TPU v7x, 32 devices: a whole 2x2x4 slice. The times are simulated.
32 devices in a mesh: parts: 2 (over y), tensor: 4 (over z), dp: 4 (over x, core).
Axes of the slice: x: 2, y: 2, z: 4, core: 2. Of those that a mesh axis runs over, the one named last changes fastest.
Arguments:
- inputs: bfloat16 [4096, 8192], P(('parts', 'dp'), 'tensor'), parts along dimension 0, may hold values from -6 to 6
- cotangent: bfloat16 [4096, 8192], P(('parts', 'dp'), 'tensor'), parts along dimension 0, may hold values from -6 to 6
- weight: bfloat16 [8192, 8192], P(None, 'tensor'), may hold values from -0.0625 to 0.0625
- down_weight_maps: bfloat16 [8192, 2048], P('tensor', 'parts'), parts along dimension 1, may hold values from -0.0625 to 0.0625
- up_weight_maps: bfloat16 [2048, 8192], P('parts', 'tensor'), parts along dimension 0, may hold values from -0.75 to 0.75
- counts: int32 [8, 16], P('parts'), parts along dimension 0, may hold values from 0 to 256, as said below
- ranks: int32 [32], P('parts'), parts along dimension 0, may hold values from 8 to 64, as said below
- owners: int32 [32], P('parts'), parts along dimension 0, may hold values from 0 to 3
Outputs:
- projected: bfloat16 [4096, 8192], P(('parts', 'dp'), 'tensor'), parts along dimension 0
- input_grad: bfloat16 [4096, 8192], P(('parts', 'dp'), 'tensor'), parts along dimension 0
- grad_a: float32 [8, 8192, 1024], P(('parts', 'dp'), 'tensor'), parts along dimension 0
- grad_b: float32 [8, 1024, 8192], P(('parts', 'dp'), None, 'tensor'), parts along dimension 0
There are 2 independent parts, one for each index of `parts`. A program takes and returns all parts, laid end to end along the dimension named above; an argument that names none is the same for every part. Nothing has to cross between parts.
Inputs may be any that keep to these rules, and one draw needn't show every extreme that they name: `counts`: each row sums to at most 512, one row to exactly 512, and all rows together to exactly 1024; some entry is exactly 256. `ranks`: each rank is 64 divided by 1, 2, 4 or 8; some trial has 64 and some 64 // 8.
All inputs are finite; a program needn't handle non-finite values.
Results may differ from a plain program's by a relative error of at most 0.0034.
Values may be sent and summed in bfloat16 or wider, within the bound.
A program may use at most 256 MiB of HBM per device.

v0:
```python
import jax
import jax.numpy as jnp
from jax import lax
from jax.sharding import PartitionSpec as P

LARGEST_RANK = 64
TRIALS = 16
LANES = 128
adapter_alpha = 16.0
TRAILING = (((1,), (1,)), ((), ()))
FIRST = (((0,), (0,)), ((), ()))


def fold_columns(values, match):
    width = values.shape[1]
    kept = jnp.where(match, values, 0.0)
    return sum((kept[:, i : i + LANES] for i in range(0, width, LANES)))


def spread_columns(folded, match):
    repeats = match.shape[1] // LANES
    return jnp.where(
        match, jnp.concatenate([folded] * repeats, axis=1), jnp.zeros((), folded.dtype)
    )


def local(inputs, cotangent, weight, down_weight_maps, up_weight_maps, counts, ranks, owners):
    slot_count, feature_local = inputs.shape
    group_count = counts.shape[0]
    width = down_weight_maps.shape[1]
    column = jnp.arange(width, dtype=jnp.int32)
    col_trial = column // LARGEST_RANK
    column_slot = column % LARGEST_RANK
    trial_ids = jnp.arange(TRIALS, dtype=jnp.int32)
    matches = col_trial[:, None] == trial_ids[None, :]
    rank_per_column = jnp.sum(jnp.where(matches, ranks[None, :], 0), axis=1)
    owner_col = jnp.sum(jnp.where(matches, owners[None, :], 0), axis=1)
    scale_per_column = jnp.where(
        column_slot < rank_per_column, adapter_alpha / rank_per_column.astype(jnp.float32), 0.0
    )
    trial_rows = jnp.sum(counts, axis=0)
    per_trial = 1.0 / jnp.maximum(trial_rows, 1).astype(jnp.float32)
    inverse_col = jnp.sum(jnp.where(matches, per_trial[None, :], 0.0), axis=1)
    cumulative = jnp.cumsum(counts, axis=1)
    group_ids = jnp.arange(group_count, dtype=jnp.int32)
    my_group = lax.axis_index("dp")
    positions = jnp.arange(slot_count, dtype=jnp.int32)
    trial_all = jnp.sum(
        (positions[None, :, None] >= cumulative[:, None, :]).astype(jnp.int32), axis=2
    )
    row_trial = jnp.sum(jnp.where((group_ids == my_group)[:, None], trial_all, 0), axis=0)
    is_live = row_trial < TRIALS
    match = row_trial[:, None] == col_trial[None, :]
    match_all = trial_all.reshape(-1)[:, None] == col_trial[None, :]
    coef = jnp.where(match, scale_per_column[None, :], 0.0)
    coef_folded = fold_columns(coef, match)
    down_part = jnp.dot(inputs, down_weight_maps, preferred_element_type=jnp.float32)
    back_part = lax.dot_general(
        cotangent, up_weight_maps, TRAILING, preferred_element_type=jnp.float32
    )
    folded = jnp.concatenate(
        [fold_columns(down_part, match), fold_columns(back_part, match)], axis=1
    )
    folded = lax.psum(folded, "tensor")
    scaled_down_f = (coef_folded * folded[:, :LANES]).astype(jnp.bfloat16)
    scaled_back_f = (coef_folded * folded[:, LANES:]).astype(jnp.bfloat16)
    all_inputs = lax.all_gather(inputs, "tensor", axis=1, tiled=True)
    mine = lax.axis_index("tensor")
    block = jnp.arange(weight.shape[0], dtype=jnp.int32) // feature_local
    frozen_back = lax.dot_general(cotangent, weight, TRAILING, preferred_element_type=jnp.float32)
    others = jnp.where((block == mine)[None, :], 0.0, frozen_back).astype(jnp.bfloat16)
    others_share = lax.psum_scatter(others, "tensor", scatter_dimension=1, tiled=True)
    own_weight = lax.dynamic_slice_in_dim(weight, mine * feature_local, feature_local, 0)
    own_share = lax.dot_general(cotangent, own_weight, TRAILING, preferred_element_type=jnp.float32)
    frozen_share = own_share + others_share.astype(jnp.float32)
    group_inputs = lax.all_gather(inputs, "dp", axis=0, tiled=True)
    group_cotangent = lax.all_gather(cotangent, "dp", axis=0, tiled=True)
    both = lax.all_gather(
        jnp.concatenate([scaled_down_f, scaled_back_f], axis=1), "dp", axis=0, tiled=True
    )
    frozen_output = jnp.dot(all_inputs, weight, preferred_element_type=jnp.float32)
    scaled_down = spread_columns(scaled_down_f, match)
    scaled_back = spread_columns(scaled_back_f, match)
    merged = frozen_output + jnp.dot(
        scaled_down, up_weight_maps, preferred_element_type=jnp.float32
    )
    projected = jnp.where(is_live[:, None], merged, 0.0).astype(jnp.bfloat16)
    adapter_in = lax.dot_general(
        scaled_back, down_weight_maps, TRAILING, preferred_element_type=jnp.float32
    )
    input_grad = jnp.where(is_live[:, None], frozen_share + adapter_in, 0.0).astype(jnp.bfloat16)
    owned = jnp.where(owner_col == my_group, inverse_col, 0.0)
    down_all = spread_columns(both[:, :LANES], match_all)
    back_all = spread_columns(both[:, LANES:], match_all)
    grad_a = lax.dot_general(group_inputs, back_all, FIRST, preferred_element_type=jnp.float32)
    grad_b = lax.dot_general(down_all, group_cotangent, FIRST, preferred_element_type=jnp.float32)
    grad_a = (grad_a * owned[None, :])[None]
    grad_b = (grad_b * owned[:, None])[None]
    return (projected, input_grad, grad_a, grad_b)


def solution(mesh):
    return jax.shard_map(
        local,
        mesh=mesh,
        in_specs=(
            P(("parts", "dp"), "tensor"),
            P(("parts", "dp"), "tensor"),
            P(None, "tensor"),
            P("tensor", "parts"),
            P("parts", "tensor"),
            P("parts", None),
            P("parts"),
            P("parts"),
        ),
        out_specs=(
            P(("parts", "dp"), "tensor"),
            P(("parts", "dp"), "tensor"),
            P(("parts", "dp"), "tensor", None),
            P(("parts", "dp"), None, "tensor"),
        ),
        check_vma=False,
    )
```

profile of v0, /device:TPU:0, one launch (start us, length us, event | category | flops | bytes accessed | tf_op | source)
XLA Modules:
  0.0 511.5 jit_solution(14548352022868119628)
XLA Ops:
  8.3 5.3 %compare_select_fusion.4 = f32[512,1024]{1,0:T(8,128)S(1)} fusion(bf16[512,2048]{1,0:T(8,128)(2,1)} %param.9, bf16[1024,2048]{1,0:T(8,128)(2,1)} %param.12, s32[1024]{0:T(1024)S(1)} %add_select_fusion.1, s32[512]{0:T(512)S(1)} %select_reduce_fusion.3), kind=kOutput, calls=%fused_computation.9 | convolution fusion | flops 2148532224 | bytes 8394752 | tf_op jit(solution)/shard_map/dot_general | solution.py:58
  13.8 2.3 compare_select_fusion.5
  17.6 40.7 %all-reduce.2.cloned.1.call-done = f32[512,256]{1,0:T(8,128)} async-done(((f32[512,256]{1,0:T(8,128)}), f32[512,256]{1,0:T(8,128)}) %all-reduce.2.cloned.1.call-update) | async-done | bytes 524304 | tf_op jit(solution)/shard_map/psum | solution.py:64
  58.2 1.1 constant_dynamic-update-slice_fusion.15
  59.3 1.8 constant_dynamic-update-slice_fusion.7
  64.0 24.4 %select_convert_fusion = bf16[512,8192]{1,0:T(8,128)(2,1)} fusion(bf16[512,2048]{1,0:T(8,128)(2,1)S(1)} %copy-done.2, bf16[8192,2048]{1,0:T(8,128)(2,1)} %param.10, pred[8192]{0:T(1024)(128)(4,1)S(1)} %fusion.23), kind=kOutput, calls=%fused_computation | convolution fusion | flops 17188257792 | bytes 44048384 | tf_op jit(solution)/shard_map/dot_general | solution.py:70
  89.6 7.7 %fusion.14 = f32[512,2048]{1,0:T(8,128)} fusion(bf16[2048,1024]{1,0:T(8,128)(2,1)} %param.11, bf16[512,1024]{1,0:T(8,128)(2,1)S(1)} %constant_dynamic-update-slice_fusion.8, s32[1024]{0:T(1024)S(1)} %add_select_fusion.1, s32[512]{0:T(512)S(1)} %select_reduce_fusion.3), kind=kOutput, calls=%fused_computation.25 | convolution fusion | flops 2148532224 | bytes 9443328 | tf_op jit(solution)/shard_map/dot_general | solution.py:88
  97.6 4.4 fusion.13
  102.0 2.0 slice_dynamic-update-slice_fusion.6
  104.0 2.0 slice_dynamic-update-slice_fusion.5
  106.0 1.9 slice_dynamic-update-slice_fusion.4
  107.9 1.9 slice_dynamic-update-slice_fusion.3
  110.6 0.9 slice_dynamic-update-slice_fusion.1
  111.5 0.9 slice_dynamic-update-slice_fusion
  112.4 1.0 slice_dynamic-update-slice_fusion.7
  119.2 19.4 %all-gather.9.cloned.1.call-done = bf16[2048,2048]{1,0:T(8,128)(2,1)} async-done(((bf16[512,2048]{1,0:T(8,128)(2,1)}), bf16[2048,2048]{1,0:T(8,128)(2,1)}) %all-gather.9.cloned.1.call-update) | async-done | bytes 8388624 | tf_op jit(solution)/shard_map/all_gather | solution.py:76
  138.6 14.9 %multiply_bitcast_fusion.1 = f32[1,2048,1024]{1,2,0:T(8,128)} fusion(bf16[2048,2048]{1,0:T(8,128)(2,1)} %all-gather.9.cloned.1.call-done, bf16[2048,1024]{1,0:T(8,128)(2,1)} %slice_dynamic-update-slice_fusion.15, f32[1024]{0:T(1024)S(1)} %compare_select_fusion.12, s32[1024]{0:T(1024)S(1)} %add_select_fusion.1, s32[2048]{0:T(1024)S(1)} %bitcast.30), kind=kOutput, calls=%fused_computation.4 | convolution fusion | flops 8596226048 | bytes 20987904 | tf_op jit(solution)/shard_map/dot_general | solution.py:95
  153.5 9.2 %copy.15 = f32[1,2048,1024]{2,1,0:T(8,128)} copy(f32[1,2048,1024]{1,2,0:T(8,128)} %multiply_bitcast_fusion.1) | data formatting | bytes 16777216
  162.7 35.6 %all-gather.11.cloned.1.call-done = bf16[2048,2048]{1,0:T(8,128)(2,1)} async-done(((bf16[512,2048]{1,0:T(8,128)(2,1)}), bf16[2048,2048]{1,0:T(8,128)(2,1)}) %all-gather.11.cloned.1.call-update) | async-done | bytes 8388624 | tf_op jit(solution)/shard_map/all_gather | solution.py:77
  198.3 14.9 %multiply_bitcast_fusion = f32[1,1024,2048]{2,1,0:T(8,128)} fusion(bf16[2048,2048]{1,0:T(8,128)(2,1)} %all-gather.11.cloned.1.call-done, bf16[2048,1024]{1,0:T(8,128)(2,1)} %get-tuple-element.19, f32[1024]{0:T(1024)S(1)} %compare_select_fusion.12, s32[1024]{0:T(1024)S(1)} %add_select_fusion.1, s32[2048]{0:T(1024)S(1)} %bitcast.31), kind=kOutput, calls=%fused_computation.3 | convolution fusion | flops 8596226048 | bytes 20987904 | tf_op jit(solution)/shard_map/dot_general | solution.py:96
  213.2 136.2 %all-gather.5.cloned.1.call-done = bf16[512,8192]{1,0:T(8,128)(2,1)} async-done(((bf16[512,2048]{1,0:T(8,128)(2,1)}), bf16[512,8192]{1,0:T(8,128)(2,1)}) %all-gather.5.cloned.1.call-update) | async-done | bytes 8388624 | tf_op jit(solution)/shard_map/all_gather | solution.py:67
  349.4 24.9 %select_convert_fusion.1 = bf16[512,2048]{1,0:T(8,128)(2,1)} fusion(f32[512,2048]{1,0:T(8,128)} %fusion.13, bf16[512,8192]{1,0:T(8,128)(2,1)} %all-gather.5.cloned.1.call-done, bf16[8192,2048]{1,0:T(8,128)(2,1)} %param.10, pred[512]{0:T(512)(128)(4,1)S(1)} %broadcast_compare_fusion), kind=kOutput, calls=%fused_computation.19 | convolution fusion | flops 17183014912 | bytes 48235008 | tf_op jit(solution)/shard_map/dot_general | solution.py:81
  374.3 120.0 %reduce-scatter.2.cloned.1.call-done = bf16[512,2048]{1,0:T(8,128)(2,1)} async-done(((bf16[512,8192]{1,0:T(8,128)(2,1)}), bf16[512,2048]{1,0:T(8,128)(2,1)}) %reduce-scatter.2.cloned.1.call-update) | async-done | bytes 2097168 | tf_op jit(solution)/shard_map/reduce_scatter | solution.py:72
  494.3 10.3 %fusion.4 = bf16[512,2048]{1,0:T(8,128)(2,1)} fusion(f32[512,2048]{1,0:T(8,128)} %fusion.14, bf16[512,2048]{1,0:T(8,128)(2,1)} %reduce-scatter.2.cloned.1.call-done, bf16[512,2048]{1,0:T(8,128)(2,1)S(1)} %copy-done.2, bf16[8192,2048]{1,0:T(8,128)(2,1)} %param.10, s32[]{:T(128)S(6)} %select_n.128, pred[512]{0:T(512)(128)(4,1)S(1)} %broadcast_compare_fusion), kind=kOutput, calls=%fused_computation.16 | convolution fusion | flops 4300210176 | bytes 18874884 | tf_op jit(solution)/shard_map/dot_general | solution.py:74
  (72 shorter events, 13.4 us)
Async XLA Ops:
  7.2 51.1 %all-reduce.2.cloned.1.call-start = ((), (), s32[]{:S(2)}) async-start(), calls=%async_computation.2 | async-start | bytes 1048576 | tf_op jit(solution)/shard_map/psum | solution.py:64
  8.3 5.5 %copy-start.1 = (bf16[512,2048]{1,0:T(8,128)(2,1)S(1)}, bf16[512,2048]{1,0:T(8,128)(2,1)}, u32[]{:S(2)}) copy-start(bf16[512,2048]{1,0:T(8,128)(2,1)} %param.8) | copy-start | bytes 6291460
  8.3 5.5 %copy-start.7 = (bf16[2048,1024]{1,0:T(8,128)(2,1)S(1)}, bf16[2048,1024]{1,0:T(8,128)(2,1)}, u32[]{:S(2)}) copy-start(bf16[2048,1024]{1,0:T(8,128)(2,1)} %param.11) | copy-start | bytes 12582916
  13.8 3.4 copy-start.5
  13.8 3.4 copy-start.6
  17.1 84.9 %all-gather.7.cloned.1.call-start = ((), (), s32[]{:S(2)}) async-start(), calls=%async_computation.4 | async-start | bytes 1310720 | tf_op jit(solution)/shard_map/all_gather | solution.py:78
  59.3 4.7 copy-start.2
  61.8 76.8 %all-gather.9.cloned.1.call-start = ((), (), s32[]{:S(2)}) async-start(), calls=%async_computation.5 | async-start | bytes 10485760 | tf_op jit(solution)/shard_map/all_gather | solution.py:76
  62.6 135.8 %all-gather.11.cloned.1.call-start = ((), (), s32[]{:S(2)}) async-start(), calls=%async_computation.6 | async-start | bytes 10485760 | tf_op jit(solution)/shard_map/all_gather | solution.py:77
  63.2 286.3 %all-gather.5.cloned.1.call-start = ((), (), s32[]{:S(2)}) async-start(), calls=%async_computation.1 | async-start | bytes 10485760 | tf_op jit(solution)/shard_map/all_gather | solution.py:67
  63.8 430.6 %reduce-scatter.2.cloned.1.call-start = ((), (), s32[]{:S(2)}) async-start(), calls=%async_computation.3 | async-start | bytes 10485760 | tf_op jit(solution)/shard_map/reduce_scatter | solution.py:72
  88.4 0.7 copy-start.4
  89.5 7.7 %copy-start.3 = (bf16[512,1024]{1,0:T(8,128)(2,1)S(1)}, bf16[512,1024]{1,0:T(8,128)(2,1)}, u32[]{:S(2)}) copy-start(bf16[512,1024]{1,0:T(8,128)(2,1)} %get-tuple-element.17) | copy-start | bytes 3145732
  89.5 8.0 %copy-start.8 = (bf16[1024,2048]{1,0:T(8,128)(2,1)S(1)}, bf16[1024,2048]{1,0:T(8,128)(2,1)}, u32[]{:S(2)}) copy-start(bf16[1024,2048]{1,0:T(8,128)(2,1)} %param.12) | copy-start | bytes 12582916
  102.0 7.8 %copy-start = (bf16[2048,256]{1,0:T(8,128)(2,1)S(1)}, bf16[2048,256]{1,0:T(8,128)(2,1)}, u32[]{:S(2)}) copy-start(bf16[2048,256]{1,0:T(8,128)(2,1)} %all-gather.7.cloned.1.call-done) | copy-start | bytes 3145732
Sparse Core Ops, SparseCore 0:
  17.2 40.9 all-reduce.1
  62.0 16.6 all-gather.6
  80.3 58.2 all-gather.8
  140.0 58.2 all-gather.10
  199.8 149.6 all-gather.4
  351.6 142.6 reduce-scatter.1
where the time goes:
time: 512 us; the launch traced here: 511 us
  waiting for transfers between devices  354 us (69%)
  matrix products  109 us (21%)
  local copies, waits for them, and re-layouts  27.7 us (5%)
  between operations  14.4 us (3%)
  other arithmetic  6.18 us (1%)
    all_gather x1, waiting for transfers between devices, local(): all_inputs = lax.all_gather(inputs, 'tensor', axis=1, tiled=True)  136 us
    reduce_scatter x1, waiting for transfers between devices, local(): lax.psum_scatter(others, 'tensor', scatter_dimension=1, tiled=True)  120 us
    psum x1, waiting for transfers between devices, local(): folded = lax.psum(folded, 'tensor')  40.7 us
    all_gather x1, waiting for transfers between devices, local(): group_cotangent = lax.all_gather(cotangent, 'dp', axis=0, tiled=True)  35.6 us
    unnamed x45, local copies, waits for them, and re-layouts  25.8 us
    dot_general x1, matrix products, local(): jnp.dot(all_inputs, weight, preferred_element_type=jnp.float32)  24.9 us
    dot_general x1, matrix products, local(): lax.dot_general(cotangent, weight, TRAILING, preferred_element_type=jnp.f...  24.4 us
    all_gather x1, waiting for transfers between devices, local(): group_inputs = lax.all_gather(inputs, 'dp', axis=0, tiled=True)  19.4 us
  transfers between devices with their start and end apart: 6, of which 5 were waited for; matrix products, arithmetic and copies ran while one was open for 23% of the time, Pallas kernels for 0%

commit v1 on v0

--- a/solution.py
+++ b/solution.py
@@ -61,7 +61,7 @@
     folded = jnp.concatenate(
         [fold_columns(down_part, match), fold_columns(back_part, match)], axis=1
     )
-    folded = lax.psum(folded, "tensor")
+    folded = jnp.sum(lax.all_gather(folded, "tensor"), axis=0)
     scaled_down_f = (coef_folded * folded[:, :LANES]).astype(jnp.bfloat16)
     scaled_back_f = (coef_folded * folded[:, LANES:]).astype(jnp.bfloat16)
     all_inputs = lax.all_gather(inputs, "tensor", axis=1, tiled=True)

time: 512 us -> 519 us (1.014)
    all_gather x0 -> x1, waiting for transfers between devices: none -> 48.3 us  [local(): folded = jnp.sum(lax.all_gather(folded, 'tensor'), axis=0)]
    psum x1 -> x0, waiting for transfers between devices: 40.7 us -> none  [local(): folded = lax.psum(folded, 'tensor')]
  transfers between devices with their start and end apart: 6 -> 6, of which waited for: 5 -> 5; matrix products, arithmetic and copies ran while one was open for 23% -> 24% of each run, Pallas kernels for 0% -> 0%
where the time goes in v1:
time: 519 us; the launch traced here: 518 us
  waiting for transfers between devices  356 us (69%)
  matrix products  109 us (21%)
  local copies, waits for them, and re-layouts  32.1 us (6%)
  between operations  14.4 us (3%)
  other arithmetic  6.57 us (1%)
    all_gather x1, waiting for transfers between devices, local(): all_inputs = lax.all_gather(inputs, 'tensor', axis=1, tiled=True)  136 us
    reduce_scatter x1, waiting for transfers between devices, local(): lax.psum_scatter(others, 'tensor', scatter_dimension=1, tiled=True)  120 us
    all_gather x1, waiting for transfers between devices, local(): folded = jnp.sum(lax.all_gather(folded, 'tensor'), axis=0)  48.3 us
    all_gather x1, waiting for transfers between devices, local(): group_cotangent = lax.all_gather(cotangent, 'dp', axis=0, tiled=True)  35.6 us
    unnamed x45, local copies, waits for them, and re-layouts  29.5 us
    dot_general x1, matrix products, local(): jnp.dot(all_inputs, weight, preferred_element_type=jnp.float32)  24.9 us
    dot_general x1, matrix products, local(): lax.dot_general(cotangent, weight, TRAILING, preferred_element_type=jnp.f...  24.5 us
    dot_general x1, matrix products, local(): lax.dot_general(group_inputs, back_all, FIRST, preferred_element_type=jnp...  14.9 us
  transfers between devices with their start and end apart: 6, of which 5 were waited for; matrix products, arithmetic and copies ran while one was open for 24% of the time, Pallas kernels for 0%

profile of v1, /device:TPU:0, one launch (start us, length us, event | category | flops | bytes accessed | tf_op | source)
XLA Modules:
  0.0 518.2 jit_solution(17458751256449526522)
XLA Ops:
  7.2 0.9 reduce_window_sum.11
  8.3 5.3 %compare_select_fusion.4 = f32[512,1024]{1,0:T(8,128)S(1)} fusion(bf16[512,2048]{1,0:T(8,128)(2,1)} %param.9, bf16[1024,2048]{1,0:T(8,128)(2,1)} %param.12, s32[1024]{0:T(1024)S(1)} %add_select_fusion.1, s32[512]{0:T(512)S(1)} %select_reduce_fusion.3), kind=kOutput, calls=%fused_computation.9 | convolution fusion | flops 2148532224 | bytes 8394752 | tf_op jit(solution)/shard_map/dot_general | solution.py:58
  13.8 2.3 compare_select_fusion.5
  17.6 48.3 %all-gather.15.cloned.1.call-done = f32[2048,256]{1,0:T(8,128)} async-done(((f32[512,256]{1,0:T(8,128)}), f32[2048,256]{1,0:T(8,128)}) %all-gather.15.cloned.1.call-update) | async-done | bytes 2097168 | tf_op jit(solution)/shard_map/all_gather | solution.py:64
  65.9 1.8 reduce_sum.66
  72.1 24.5 %select_convert_fusion = bf16[512,8192]{1,0:T(8,128)(2,1)} fusion(bf16[512,2048]{1,0:T(8,128)(2,1)S(1)} %copy-done.2, bf16[8192,2048]{1,0:T(8,128)(2,1)} %param.10, pred[8192]{0:T(1024)(128)(4,1)S(1)} %fusion.23), kind=kOutput, calls=%fused_computation | convolution fusion | flops 17188257792 | bytes 44048384 | tf_op jit(solution)/shard_map/dot_general | solution.py:70
  102.1 7.1 %fusion.14 = f32[512,2048]{1,0:T(8,128)} fusion(bf16[2048,1024]{1,0:T(8,128)(2,1)} %param.11, bf16[512,1024]{1,0:T(8,128)(2,1)} %constant_dynamic-update-slice_fusion.8, s32[1024]{0:T(1024)S(1)} %add_select_fusion.1, s32[512]{0:T(512)S(1)} %select_reduce_fusion.3), kind=kOutput, calls=%fused_computation.25 | convolution fusion | flops 2148532224 | bytes 9443328 | tf_op jit(solution)/shard_map/dot_general | solution.py:88
  109.5 4.4 fusion.13
  113.9 2.0 slice_dynamic-update-slice_fusion.6
  115.9 1.9 slice_dynamic-update-slice_fusion.5
  117.9 1.9 slice_dynamic-update-slice_fusion.4
  119.8 1.9 slice_dynamic-update-slice_fusion.3
  122.6 0.9 slice_dynamic-update-slice_fusion.1
  123.4 0.9 slice_dynamic-update-slice_fusion
  124.3 1.0 slice_dynamic-update-slice_fusion.7
  131.2 14.2 %all-gather.11.cloned.1.call-done = bf16[2048,2048]{1,0:T(8,128)(2,1)} async-done(((bf16[512,2048]{1,0:T(8,128)(2,1)}), bf16[2048,2048]{1,0:T(8,128)(2,1)}) %all-gather.11.cloned.1.call-update) | async-done | bytes 8388624 | tf_op jit(solution)/shard_map/all_gather | solution.py:76
  145.4 14.9 %multiply_bitcast_fusion.1 = f32[1,2048,1024]{1,2,0:T(8,128)} fusion(bf16[2048,2048]{1,0:T(8,128)(2,1)} %all-gather.11.cloned.1.call-done, bf16[2048,1024]{1,0:T(8,128)(2,1)} %slice_dynamic-update-slice_fusion.15, f32[1024]{0:T(1024)S(1)} %compare_select_fusion.12, s32[1024]{0:T(1024)S(1)} %add_select_fusion.1, s32[2048]{0:T(1024)S(1)} %bitcast.32), kind=kOutput, calls=%fused_computation.4 | convolution fusion | flops 8596226048 | bytes 20987904 | tf_op jit(solution)/shard_map/dot_general | solution.py:95
  160.3 9.2 %copy.15 = f32[1,2048,1024]{2,1,0:T(8,128)} copy(f32[1,2048,1024]{1,2,0:T(8,128)} %multiply_bitcast_fusion.1) | data formatting | bytes 16777216
  169.5 35.6 %all-gather.13.cloned.1.call-done = bf16[2048,2048]{1,0:T(8,128)(2,1)} async-done(((bf16[512,2048]{1,0:T(8,128)(2,1)}), bf16[2048,2048]{1,0:T(8,128)(2,1)}) %all-gather.13.cloned.1.call-update) | async-done | bytes 8388624 | tf_op jit(solution)/shard_map/all_gather | solution.py:77
  205.1 14.9 %multiply_bitcast_fusion = f32[1,1024,2048]{2,1,0:T(8,128)} fusion(bf16[2048,2048]{1,0:T(8,128)(2,1)} %all-gather.13.cloned.1.call-done, bf16[2048,1024]{1,0:T(8,128)(2,1)} %get-tuple-element.19, f32[1024]{0:T(1024)S(1)} %compare_select_fusion.12, s32[1024]{0:T(1024)S(1)} %add_select_fusion.1, s32[2048]{0:T(1024)S(1)} %bitcast.33), kind=kOutput, calls=%fused_computation.3 | convolution fusion | flops 8596226048 | bytes 20987904 | tf_op jit(solution)/shard_map/dot_general | solution.py:96
  220.0 136.2 %all-gather.7.cloned.1.call-done = bf16[512,8192]{1,0:T(8,128)(2,1)} async-done(((bf16[512,2048]{1,0:T(8,128)(2,1)}), bf16[512,8192]{1,0:T(8,128)(2,1)}) %all-gather.7.cloned.1.call-update) | async-done | bytes 8388624 | tf_op jit(solution)/shard_map/all_gather | solution.py:67
  356.2 24.9 %select_convert_fusion.1 = bf16[512,2048]{1,0:T(8,128)(2,1)} fusion(f32[512,2048]{1,0:T(8,128)} %fusion.13, bf16[512,8192]{1,0:T(8,128)(2,1)} %all-gather.7.cloned.1.call-done, bf16[8192,2048]{1,0:T(8,128)(2,1)} %param.10, pred[512]{0:T(512)(128)(4,1)S(1)} %broadcast_compare_fusion), kind=kOutput, calls=%fused_computation.19 | convolution fusion | flops 17183014912 | bytes 48235008 | tf_op jit(solution)/shard_map/dot_general | solution.py:81
  381.1 120.0 %reduce-scatter.2.cloned.1.call-done = bf16[512,2048]{1,0:T(8,128)(2,1)} async-done(((bf16[512,8192]{1,0:T(8,128)(2,1)}), bf16[512,2048]{1,0:T(8,128)(2,1)}) %reduce-scatter.2.cloned.1.call-update) | async-done | bytes 2097168 | tf_op jit(solution)/shard_map/reduce_scatter | solution.py:72
  501.1 10.3 %fusion.4 = bf16[512,2048]{1,0:T(8,128)(2,1)} fusion(f32[512,2048]{1,0:T(8,128)} %fusion.14, bf16[512,2048]{1,0:T(8,128)(2,1)} %reduce-scatter.2.cloned.1.call-done, bf16[512,2048]{1,0:T(8,128)(2,1)S(1)} %copy-done.2, bf16[8192,2048]{1,0:T(8,128)(2,1)} %param.10, s32[]{:T(128)S(6)} %select_n.128, pred[512]{0:T(512)(128)(4,1)S(1)} %broadcast_compare_fusion), kind=kOutput, calls=%fused_computation.16 | convolution fusion | flops 4300210176 | bytes 18874884 | tf_op jit(solution)/shard_map/dot_general | solution.py:74
  (73 shorter events, 18.4 us)
Async XLA Ops:
  7.2 58.7 %all-gather.15.cloned.1.call-start = ((), (), s32[]{:S(2)}) async-start(), calls=%async_computation.6 | async-start | bytes 2621440 | tf_op jit(solution)/shard_map/all_gather | solution.py:64
  8.3 5.5 %copy-start.1 = (bf16[512,2048]{1,0:T(8,128)(2,1)S(1)}, bf16[512,2048]{1,0:T(8,128)(2,1)}, u32[]{:S(2)}) copy-start(bf16[512,2048]{1,0:T(8,128)(2,1)} %param.8) | copy-start | bytes 6291460
  8.3 5.5 %copy-start.7 = (bf16[2048,1024]{1,0:T(8,128)(2,1)S(1)}, bf16[2048,1024]{1,0:T(8,128)(2,1)}, u32[]{:S(2)}) copy-start(bf16[2048,1024]{1,0:T(8,128)(2,1)} %param.11) | copy-start | bytes 12582916
  13.8 3.4 copy-start.5
  13.8 3.4 copy-start.6
  17.1 96.8 %all-gather.9.cloned.1.call-start = ((), (), s32[]{:S(2)}) async-start(), calls=%async_computation.3 | async-start | bytes 1310720 | tf_op jit(solution)/shard_map/all_gather | solution.py:78
  68.5 3.6 copy-start.2
  69.9 75.5 %all-gather.11.cloned.1.call-start = ((), (), s32[]{:S(2)}) async-start(), calls=%async_computation.4 | async-start | bytes 10485760 | tf_op jit(solution)/shard_map/all_gather | solution.py:76
  70.6 134.5 %all-gather.13.cloned.1.call-start = ((), (), s32[]{:S(2)}) async-start(), calls=%async_computation.5 | async-start | bytes 10485760 | tf_op jit(solution)/shard_map/all_gather | solution.py:77
  71.2 285.0 %all-gather.7.cloned.1.call-start = ((), (), s32[]{:S(2)}) async-start(), calls=%async_computation.1 | async-start | bytes 10485760 | tf_op jit(solution)/shard_map/all_gather | solution.py:67
  71.8 429.3 %reduce-scatter.2.cloned.1.call-start = ((), (), s32[]{:S(2)}) async-start(), calls=%async_computation.2 | async-start | bytes 10485760 | tf_op jit(solution)/shard_map/reduce_scatter | solution.py:72
  96.6 0.7 copy-start.4
  102.1 7.1 %copy-start.3 = (bf16[512,1024]{1,0:T(8,128)(2,1)S(1)}, bf16[512,1024]{1,0:T(8,128)(2,1)}, u32[]{:S(2)}) copy-start(bf16[512,1024]{1,0:T(8,128)(2,1)} %get-tuple-element.17) | copy-start | bytes 3145732
  102.1 7.4 %copy-start.8 = (bf16[1024,2048]{1,0:T(8,128)(2,1)S(1)}, bf16[1024,2048]{1,0:T(8,128)(2,1)}, u32[]{:S(2)}) copy-start(bf16[1024,2048]{1,0:T(8,128)(2,1)} %param.12) | copy-start | bytes 12582916
  113.9 7.8 %copy-start = (bf16[2048,256]{1,0:T(8,128)(2,1)S(1)}, bf16[2048,256]{1,0:T(8,128)(2,1)}, u32[]{:S(2)}) copy-start(bf16[2048,256]{1,0:T(8,128)(2,1)} %all-gather.9.cloned.1.call-done) | copy-start | bytes 3145732
Sparse Core Ops, SparseCore 0:
  17.2 48.6 all-gather.14
  70.0 15.4 all-gather.8
  87.1 58.2 all-gather.10
  146.8 58.2 all-gather.12
  206.5 149.6 all-gather.6
  358.4 142.6 reduce-scatter.1
